TPU v7x, 256 devices: a whole 4x4x8 slice. The times are simulated.
256 devices in a mesh: section: 16 (over z_hi, x, core), blk: 16 (over y, z_lo).
Axes of the slice: x: 4, y: 4, z: 8 (z_hi: 2, z_lo: 4; z = z_hi * 4 + z_lo), core: 2. Of those that a mesh axis runs over, the one named last changes fastest.
Arguments:
- queries: bfloat16 [16, 2048, 4096], P('section', 'blk'), may hold values from -6 to 6
- key_heads: bfloat16 [16, 2048, 512], P('section', 'blk'), may hold values from -6 to 6
- value_per_head: bfloat16 [16, 2048, 512], P('section', 'blk'), may hold values from -6 to 6
- out_grads: bfloat16 [16, 2048, 4096], P('section', 'blk'), may hold values from -6 to 6
- segment_ids: int32 [16, 2048], P('section', 'blk'), may hold values from 0 to 127, never falling along the last dimension, each value on 1 to 64 neighbouring positions
- block_lists: int32 [16, 16, 4], P('section', 'blk'), may hold values from 0 to 15, as said below
- list_counts: int32 [16, 16], P('section', 'blk'), may hold values from 1 to 4, as said below
Outputs:
- grad_queries: bfloat16 [16, 2048, 4096], P('section', 'blk')
- grad_keys: bfloat16 [16, 2048, 512], P('section', 'blk')
- grad_values: bfloat16 [16, 2048, 512], P('section', 'blk')
Inputs may be any that keep to these rules, and one draw needn't show every extreme that they name: `block_lists`: entry 0 of row b is b itself; for b >= 1 entry 1 is block 0; entries 2 to list_counts - 1 are distinct blocks between 1 and b - 1; entries from list_counts on repeat b. `list_counts`: at least 2 for every query block after the first; the last query block of every micro-batch uses all 4 slots.
All inputs are finite; a program needn't handle non-finite values.
Results may differ from a plain program's by a relative error of at most 0.0051.
Values may be sent and summed in bfloat16 or wider, within the bound.
A program may use at most 64 MiB of HBM per device.

v0:
```python
import math

import jax
import jax.numpy as jnp
from jax import lax
from jax.sharding import PartitionSpec as P

QUERY_HEADS = 32
KEY_VALUE_HEADS = 4
HEAD_SIZE = 128
MASK_BLOCK_SIZE = 128
LIST = 4


NEG_FILL = -1e30


def from_behind(value, axis, by):
    devices = lax.axis_size(axis)
    return lax.ppermute(value, axis, [(i, (i + by) % devices) for i in range(devices)])


def allowed_mask(block_ids, listed_count, query_block, query_segs):
    slot_ok = jnp.arange(LIST, dtype=jnp.int32) < listed_count
    own_block = block_ids == query_block
    positions = jnp.arange(MASK_BLOCK_SIZE, dtype=jnp.int32)
    causal = (positions[None, :] <= positions[:, None]) & (
        query_segs[None, :] == query_segs[:, None]
    )
    earlier = block_ids < query_block
    return slot_ok[None, :, None] & jnp.where(
        own_block[None, :, None], causal[:, None, :], earlier[None, :, None]
    )


def group_terms(query_row_slice, gradient_row_slice, key_rows, value_rows, allowed):
    scale_factor = 1.0 / math.sqrt(HEAD_SIZE)
    scores = (
        jnp.einsum("ihd,ljd->hilj", query_row_slice, key_rows, preferred_element_type=jnp.float32)
        * scale_factor
    )
    scores = jnp.where(allowed[None], scores, NEG_FILL)
    largest = jnp.max(scores, axis=(2, 3), keepdims=True)
    weights = jnp.where(allowed[None], jnp.exp(scores - largest), 0.0)
    probs_full = weights / jnp.sum(weights, axis=(2, 3), keepdims=True)
    dprobs = jnp.einsum(
        "ihd,ljd->hilj", gradient_row_slice, value_rows, preferred_element_type=jnp.float32
    )
    row_delta = jnp.sum(probs_full * dprobs, axis=(2, 3), keepdims=True)
    dscores = (probs_full * (dprobs - row_delta)).astype(jnp.bfloat16)
    probs_half = probs_full.astype(jnp.bfloat16)
    query_grad = (
        jnp.einsum("hilj,ljd->ihd", dscores, key_rows, preferred_element_type=jnp.float32)
        * scale_factor
    )
    key_grad = (
        jnp.einsum("hilj,ihd->ljd", dscores, query_row_slice, preferred_element_type=jnp.float32)
        * scale_factor
    )
    value_grad = jnp.einsum(
        "hilj,ihd->ljd", probs_half, gradient_row_slice, preferred_element_type=jnp.float32
    )
    return (query_grad, key_grad, value_grad)


def per_device(
    queries, key_heads, value_per_head, out_grads, segment_ids, block_lists, list_counts
):
    local_blocks = block_lists.shape[1]
    blk_count = lax.axis_size("blk")
    blocks_all = blk_count * local_blocks
    first_local = lax.axis_index("blk") * local_blocks
    heads_per_group = QUERY_HEADS // KEY_VALUE_HEADS
    key_value_width = KEY_VALUE_HEADS * HEAD_SIZE
    ids_all = block_lists[0]
    flat_ids = ids_all.reshape(-1)
    whole_keys, whole_values = (
        lax.all_gather(key_heads, "blk", axis=1, tiled=True),
        lax.all_gather(value_per_head, "blk", axis=1, tiled=True),
    )
    listed_k = whole_keys[0].reshape(blocks_all, MASK_BLOCK_SIZE, key_value_width)[flat_ids]
    listed_v = whole_values[0].reshape(blocks_all, MASK_BLOCK_SIZE, key_value_width)[flat_ids]
    query_all = queries[0]
    grads_all = out_grads[0]
    segs_all = segment_ids[0]
    counts_all = list_counts[0]
    query_block = first_local + 0
    row_hi = MASK_BLOCK_SIZE
    allowed = allowed_mask(ids_all[0], counts_all[0], query_block, segs_all)
    query_parts = []
    key_parts = []
    value_parts = []
    for shared_key_head in range(KEY_VALUE_HEADS):
        col_lo = shared_key_head * heads_per_group * HEAD_SIZE
        col_hi = col_lo + heads_per_group * HEAD_SIZE
        query_row_slice = query_all[0:row_hi, col_lo:col_hi].reshape(
            MASK_BLOCK_SIZE, heads_per_group, HEAD_SIZE
        )
        gradient_row_slice = grads_all[0:row_hi, col_lo:col_hi].reshape(
            MASK_BLOCK_SIZE, heads_per_group, HEAD_SIZE
        )
        head_keys = listed_k[:, :, shared_key_head * HEAD_SIZE : (shared_key_head + 1) * HEAD_SIZE]
        head_values = listed_v[
            :, :, shared_key_head * HEAD_SIZE : (shared_key_head + 1) * HEAD_SIZE
        ]
        query_grad, key_grad, value_grad = group_terms(
            query_row_slice, gradient_row_slice, head_keys, head_values, allowed
        )
        query_parts.append(query_grad.reshape(MASK_BLOCK_SIZE, heads_per_group * HEAD_SIZE))
        key_parts.append(key_grad)
        value_parts.append(value_grad)
    query_parts_all = jnp.concatenate(query_parts, axis=1).astype(jnp.bfloat16)
    grad_tiles = jnp.concatenate(key_parts + value_parts, axis=2)
    query_gradient_rows = query_parts_all[None]
    placement = (jnp.arange(blocks_all, dtype=jnp.int32)[:, None] == flat_ids[None, :]).astype(
        jnp.float32
    )
    term_all = jnp.einsum("cn,nrw->crw", placement, grad_tiles, precision=lax.Precision.HIGHEST)
    summed = lax.psum_scatter(
        term_all.reshape(blocks_all * MASK_BLOCK_SIZE, 2 * key_value_width),
        "blk",
        scatter_dimension=0,
        tiled=True,
    )
    summed_half = summed.astype(jnp.bfloat16)
    key_grads = summed_half[:, :key_value_width][None]
    value_grads = summed_half[:, key_value_width:][None]
    grad_queries, grad_keys, grad_values = from_behind(
        (query_gradient_rows, key_grads, value_grads), "section", -1
    )
    return (grad_queries, grad_keys, grad_values)


def solution(mesh):
    in_specs = (
        P("section", "blk", None),
        P("section", "blk", None),
        P("section", "blk", None),
        P("section", "blk", None),
        P("section", "blk"),
        P("section", "blk", None),
        P("section", "blk"),
    )
    out_specs = (P("section", "blk", None), P("section", "blk", None), P("section", "blk", None))
    return jax.shard_map(
        per_device, mesh=mesh, in_specs=in_specs, out_specs=out_specs, check_vma=False
    )
```

profile of v0, /device:TPU:7, one launch (start us, length us, event | category | flops | bytes accessed | tf_op | source)
XLA Modules:
  0.0 443.1 jit_solution(12771451435008800897)
XLA Ops:
  7.2 0.7 all-gather.3.cloned.1.call-update
  8.0 0.7 all-gather.5.cloned.1.call-update
  9.4 1.6 copy.22
  11.0 0.7 copy.24
  12.2 78.9 %all-gather.3.cloned.1.call-done = bf16[1,2048,512]{2,1,0:T(8,128)(2,1)} async-done(((bf16[1,128,512]{2,1,0:T(8,128)(2,1)}), bf16[1,2048,512]{2,1,0:T(8,128)(2,1)}) %all-gather.3.cloned.1.call-update) | async-done | bytes 2097168 | tf_op jit(solution)/shard_map/all_gather | solution.py:78
  91.0 2.2 gather_fusion
  93.2 86.1 %all-gather.5.cloned.1.call-done = bf16[1,2048,512]{2,1,0:T(8,128)(2,1)} async-done(((bf16[1,128,512]{2,1,0:T(8,128)(2,1)}), bf16[1,2048,512]{2,1,0:T(8,128)(2,1)}) %all-gather.5.cloned.1.call-update) | async-done | bytes 2097168 | tf_op jit(solution)/shard_map/all_gather | solution.py:79
  179.3 2.2 gather_fusion.1
  181.4 0.4 fusion.50
  181.9 0.4 fusion.51
  182.3 0.4 fusion.49
  182.7 0.4 fusion.44
  183.2 0.5 fusion.12
  183.6 0.5 fusion.17
  184.1 0.7 fusion.38
  184.8 1.7 fusion.9
  186.5 0.5 fusion.19
  187.0 0.7 fusion.36
  187.7 1.8 fusion.6
  189.6 0.7 fusion.32
  190.3 0.7 fusion.34
  191.0 1.4 fusion.3
  192.4 2.4 fusion.11
  194.8 0.4 fusion.64
  195.3 0.4 fusion.67
  195.8 0.4 fusion.65
  196.2 0.7 fusion.5
  196.9 0.4 fusion.66
  197.6 0.3 fusion.42
  197.9 0.3 fusion.41
  198.2 0.3 fusion.40
  199.4 4.0 fusion.54
  203.4 8.3 %copy.44 = f32[16,128,1024]{2,1,0:T(8,128)} copy(f32[16,128,1024]{2,0,1:T(8,128)S(1)} %fusion.54) | data formatting | bytes 16777216 | tf_op jit(solution)/shard_map/cn,nrw->crw/dot_general | solution.py:118
  211.8 1.2 fusion.31
  213.0 0.9 copy.40
  213.9 1.2 fusion.28
  215.1 0.9 copy.43
  216.0 1.3 fusion.29
  217.4 1.2 fusion.30
  218.9 9.5 %collective-permute-start = (bf16[1,128,4096]{2,1,0:T(8,128)(2,1)S(1)}, bf16[1,128,4096]{2,1,0:T(8,128)(2,1)S(1)}, u32[]{:S(2)}, u32[]{:S(2)}) collective-permute-start(bf16[1,128,4096]{2,1,0:T(8,128)(2,1)S(1)} %pad_maximum_fusion), channel_id=1, source_target_pairs={{0,240},{16,0},{32,16},{48,32},{64,48},{80,64},{96,80},{112,96},{1... | collective-permute-start | bytes 3145736 | tf_op jit(solution)/shard_map/ppermute | solution.py:20
  228.4 179.4 %reduce-scatter.2.cloned.1.call-done = f32[128,1024]{1,0:T(8,128)} async-done(((f32[2048,1024]{1,0:T(8,128)}), f32[128,1024]{1,0:T(8,128)}) %reduce-scatter.2.cloned.1.call-update) | async-done | bytes 524304 | tf_op jit(solution)/shard_map/reduce_scatter | solution.py:119
  407.8 1.1 convert_element_type.44
  408.9 0.9 collective-permute-start.2
  410.0 22.9 %collective-permute-done.2 = bf16[1,128,512]{2,1,0:T(8,128)(2,1)S(1)} collective-permute-done((bf16[1,128,512]{2,1,0:T(8,128)(2,1)S(1)}, bf16[1,128,512]{2,1,0:T(8,128)(2,1)S(1)}, u32[]{:S(2)}, u32[]{:S(2)}) %collective-permute-start.2) | collective-permute-done | bytes 131104 | tf_op jit(solution)/shard_map/ppermute | solution.py:20
  432.9 1.4 collective-permute-done.1
  434.3 1.0 copy.116
  435.2 0.7 copy.117
  435.9 0.7 copy.118
  (51 shorter events, 2.3 us)
Async XLA Ops:
  7.2 3.8 copy-start.9
  7.2 83.8 %all-gather.3.cloned.1.call-start = ((), (), s32[]{:S(2)}) async-start(), calls=%async_computation.1 | async-start | bytes 2228224 | tf_op jit(solution)/shard_map/all_gather | solution.py:78
  7.9 171.4 %all-gather.5.cloned.1.call-start = ((), (), s32[]{:S(2)}) async-start(), calls=%async_computation.2 | async-start | bytes 2228224 | tf_op jit(solution)/shard_map/all_gather | solution.py:79
  8.7 399.2 %reduce-scatter.2.cloned.1.call-start = ((), (), s32[]{:S(2)}) async-start(), calls=%async_computation.3 | async-start | bytes 8912896 | tf_op jit(solution)/shard_map/reduce_scatter | solution.py:119
  9.4 2.3 copy-start.13
  9.4 2.4 copy-start.12
  12.0 169.8 %copy-start.5 = (bf16[128,1024]{0,1:T(8,128)(2,1)}, bf16[128,1024]{0,1:T(8,128)(2,1)S(1)}, u32[]{:S(2)}) copy-start(bf16[128,1024]{0,1:T(8,128)(2,1)S(1)} %get-tuple-element.12) | copy-start | bytes 786436
  12.1 170.2 %copy-start.3 = (bf16[128,1024]{0,1:T(8,128)(2,1)}, bf16[128,1024]{0,1:T(8,128)(2,1)S(1)}, u32[]{:S(2)}) copy-start(bf16[128,1024]{0,1:T(8,128)(2,1)S(1)} %get-tuple-element.14) | copy-start | bytes 786436
  12.1 171.1 %copy-start.7 = (bf16[128,1024]{0,1:T(8,128)(2,1)}, bf16[128,1024]{0,1:T(8,128)(2,1)S(1)}, u32[]{:S(2)}) copy-start(bf16[128,1024]{0,1:T(8,128)(2,1)S(1)} %get-tuple-element.15) | copy-start | bytes 786436
  93.2 90.0 %copy-start.2 = (bf16[4,128,512]{2,1,0:T(8,128)(2,1)}, bf16[4,128,512]{2,1,0:T(8,128)(2,1)S(1)}, u32[]{:S(2)}) copy-start(bf16[4,128,512]{2,1,0:T(8,128)(2,1)S(1)} %gather_fusion) | copy-start | bytes 1572868
  192.4 2.5 copy-start.8
  192.4 2.9 copy-start.6
  194.8 1.0 copy-start.4
  196.9 1.7 copy-start
  213.0 3.0 copy-start.1
  216.0 2.9 copy-start.10
  217.3 1.6 copy-start.11
  218.9 191.1 %collective-permute-start = (bf16[1,128,4096]{2,1,0:T(8,128)(2,1)S(1)}, bf16[1,128,4096]{2,1,0:T(8,128)(2,1)S(1)}, u32[]{:S(2)}, u32[]{:S(2)}) collective-permute-start(bf16[1,128,4096]{2,1,0:T(8,128)(2,1)S(1)} %pad_maximum_fusion), channel_id=1, source_target_pairs={{0,240},{16,0},{32,16},{48,32},{64,48},{80,64},{96,80},{112,96},{1... | collective-permute-start | bytes 3145736 | tf_op jit(solution)/shard_map/ppermute | solution.py:20
  408.9 23.9 %collective-permute-start.2 = (bf16[1,128,512]{2,1,0:T(8,128)(2,1)S(1)}, bf16[1,128,512]{2,1,0:T(8,128)(2,1)S(1)}, u32[]{:S(2)}, u32[]{:S(2)}) collective-permute-start(bf16[1,128,512]{2,1,0:T(8,128)(2,1)S(1)} %get-tuple-element.20), channel_id=1, source_target_pairs={{0,240},{16,0},{32,16},{48,32},{64,48},{80,64},{96,80},{112,96},{1... | collective-permute-start | bytes 393224 | tf_op jit(solution)/shard_map/ppermute | solution.py:20
  409.9 24.4 %collective-permute-start.1 = (bf16[1,128,512]{2,1,0:T(8,128)(2,1)S(1)}, bf16[1,128,512]{2,1,0:T(8,128)(2,1)S(1)}, u32[]{:S(2)}, u32[]{:S(2)}) collective-permute-start(bf16[1,128,512]{2,1,0:T(8,128)(2,1)S(1)} %get-tuple-element.21), channel_id=1, source_target_pairs={{0,240},{16,0},{32,16},{48,32},{64,48},{80,64},{96,80},{112,96},{1... | collective-permute-start | bytes 393224 | tf_op jit(solution)/shard_map/ppermute | solution.py:20
Sparse Core Ops, SparseCore 0:
  9.8 81.1 all-gather.2
  92.8 86.4 all-gather.4
  211.9 195.9 reduce-scatter.1
where the time goes:
time: 443 us
  waiting for transfers between devices  370 us (84%)
  matrix products  20.5 us (5%)
  local copies, waits for them, and re-layouts  20.4 us (5%)
  between operations  14.9 us (3%)
  starting transfers between devices  10.7 us (2%)
  other arithmetic  6.55 us (1%)
    reduce_scatter x1, waiting for transfers between devices, per_device(): lax.psum_scatter(term_all.reshape(blocks_all * MASK_BLOCK_SIZE, 2 * key_v...  179 us
    all_gather x1, waiting for transfers between devices, per_device(): lax.all_gather(value_per_head, 'blk', axis=1, tiled=True)  86.1 us
    all_gather x1, waiting for transfers between devices, per_device(): lax.all_gather(key_heads, 'blk', axis=1, tiled=True)  78.9 us
    ppermute x3, waiting for transfers between devices, from_behind(): lax.ppermute(value, axis, [(i, (i + by) % devices) for i in range(devices)])  24.3 us
    ppermute x3, starting transfers between devices, from_behind(): lax.ppermute(value, axis, [(i, (i + by) % devices) for i in range(devices)])  10.6 us
  transfers between devices with their start and end apart: 6, of which 5 were waited for; matrix products, arithmetic and copies ran while one was open for 3% of the time, Pallas kernels for 0%

commit v1 on v0

v1 whole, which is shorter than its diff:
```python
import functools
import math

import jax
import jax.numpy as jnp
from jax import lax
from jax.experimental import pallas as pl
from jax.experimental.pallas import tpu as pltpu
from jax.sharding import PartitionSpec as P

QUERY_HEADS = 32
GROUPS = 4
HEAD = 128
BLOCK = 128
LIST = 4
PER_GROUP = QUERY_HEADS // GROUPS
GROUP_WIDTH = PER_GROUP * HEAD
ROWS = 4
COLS = 4
NEG_FILL = -1e30
SCALE = 1.0 / math.sqrt(HEAD)
EXP2_SCALE = SCALE * math.log2(math.e)
MESH = pl.DeviceIdType.MESH


def body(
    lists, counts, segs, keys, values, queries, grads,
    dq_out, dk_out, dv_out,
    row0, row1, row2, row3, far0, far1, far2, far3,
    id_tile, id_in, id_smem,
    q_buf, g_buf, stage, mask0, kc, vc, kt, dk_acc, dv_acc, dq_buf,
    y_send, y_in, row_acc, l_send, l_in, r_send, r_in, fin,
    id_ss, id_rs, id_ls, qg_s,
    zs, zr, ys, yr, bs, br, rys, ryr, ls, lr, rs, rr, dqs, dqr, dks, dkr,
):
    rowkv = (row0, row1, row2, row3)
    far = (far0, far1, far2, far3)
    sec = lax.axis_index("section")
    blk = lax.axis_index("blk")
    sections = lax.axis_size("section")
    y = blk // COLS
    z = lax.rem(blk, COLS)

    def at(yy, zz):
        return (sec, yy * COLS + zz)

    def remote(src, dst, ssem, rsem, dev):
        return pltpu.make_async_remote_copy(
            src_ref=src, dst_ref=dst, send_sem=ssem, recv_sem=rsem,
            device_id=dev, device_id_type=MESH,
        )

    here = (sec, blk)
    behind = (lax.rem(sec + sections - 1, sections), blk)
    ahead = (lax.rem(sec + 1, sections), blk)

    q_copy = pltpu.make_async_copy(queries.at[0], q_buf, qg_s.at[0])
    g_copy = pltpu.make_async_copy(grads.at[0], g_buf, qg_s.at[1])
    q_copy.start()
    g_copy.start()

    barrier = pltpu.get_barrier_semaphore()
    peers = [behind, ahead]
    for d in (1, 3):
        peers.append(at(y, lax.rem(z + d, COLS)))
    for d in (1, 2, 3):
        peers.append(at(lax.rem(y + d, ROWS), z))
    for p in peers:
        pl.semaphore_signal(barrier, inc=1, device_id=p, device_id_type=MESH)

    lanes = lax.broadcasted_iota(jnp.int32, (8, BLOCK), 0)
    tile = jnp.zeros((8, BLOCK), jnp.int32)
    for s in range(LIST):
        tile = jnp.where(lanes == s, lists[s], tile)
    id_tile[...] = tile
    for g in range(GROUPS):
        for zz in range(COLS):
            @pl.when(z == zz)
            def _(g=g, zz=zz):
                rowkv[g][zz, :BLOCK] = keys[0, :, g * HEAD:(g + 1) * HEAD]
                rowkv[g][zz, BLOCK:] = values[0, :, g * HEAD:(g + 1) * HEAD]

    pl.semaphore_wait(barrier, len(peers))

    for lo in range(ROWS - 1):
        @pl.when(lo < y)
        def _(lo=lo):
            remote(id_tile, id_in.at[y], id_ss.at[lo], id_rs.at[y], at(lo, z)).start()

    def hop(g, src, to):
        return remote(rowkv[g].at[src], rowkv[g].at[src], zs.at[g, src, to], zr.at[g, src],
                      at(y, z + 1) if to else at(y, z - 1))

    for g in range(GROUPS):
        for zz in range(COLS):
            @pl.when(z == zz)
            def _(g=g, zz=zz):
                if zz < COLS - 1:
                    hop(g, zz, 1).start()
                if zz > 0:
                    hop(g, zz, 0).start()

    seg_row = jnp.broadcast_to(segs[...].astype(jnp.float32), (BLOCK, BLOCK))
    seg_col = seg_row.T
    key_pos = lax.broadcasted_iota(jnp.int32, (BLOCK, BLOCK), 0)
    query_pos = lax.broadcasted_iota(jnp.int32, (BLOCK, BLOCK), 1)
    mask0[...] = jnp.where((key_pos <= query_pos) & (seg_row == seg_col), 1.0, 0.0)

    for hi in range(1, ROWS):
        @pl.when(hi > y)
        def _(hi=hi):
            remote(id_tile, id_in.at[hi], id_ss.at[0], id_rs.at[hi], here).wait_recv()
            c = pltpu.make_async_copy(id_in.at[hi], id_smem.at[hi], id_ls.at[hi])
            c.start()
            c.wait()

    own_id = [lists[s] for s in range(LIST)]
    count = counts[0]

    def gather_row(g):
        for zz in range(COLS):
            @pl.when(z == zz)
            def _(zz=zz):
                for dist in range(1, COLS):
                    for src, onward in ((zz - dist, 1), (zz + dist, 0)):
                        if 0 <= src < COLS:
                            hop(g, src, onward).wait_recv()
                            if onward and zz < COLS - 1 or not onward and zz > 0:
                                hop(g, src, onward).start()

    def far_copy(g, lo, hi):
        return remote(stage.at[g, hi - 1], far[g].at[lo, pl.ds(1, 2)], ys.at[g, lo, hi - 1],
                      yr.at[g, lo], at(hi, z))

    def first_copy(g, hi):
        return remote(rowkv[g].at[0], far[g].at[0, 0], bs.at[g, hi - 1], br.at[g], at(hi, z))

    def send_listed(g):
        @pl.when(y == 0)
        def _():
            for hi in range(1, ROWS):
                first_copy(g, hi).start()
        for lo in range(ROWS - 1):
            @pl.when(y == lo)
            def _(lo=lo):
                for hi in sorted(range(lo + 1, ROWS), reverse=True):
                    for s in (2, 3):
                        idx = lax.rem(id_smem[hi, s, 0], COLS)
                        stage[g, hi - 1, s - 2] = rowkv[g][idx]
                    far_copy(g, lo, hi).start()

    def pick(g, s):
        block = own_id[s]
        r, c = block // COLS, lax.rem(block, COLS)
        near = rowkv[g][c]
        away = far[g][jnp.minimum(r, ROWS - 2), s - 1]
        return jnp.where(r == y, near, away)

    def y_copy(g, lo, hi):
        src, dst = (y_send.at[g], y_in.at[g, hi - 1]) if lo == 0 else (
            y_send.at[g, pl.ds(1, 2)], y_in.at[g, hi - 1, pl.ds(1, 2)])
        return remote(src, dst, rys.at[g, lo], ryr.at[g, hi - 1], at(lo, z))

    def dq_copy(g):
        cols = pl.ds(g * GROUP_WIDTH, GROUP_WIDTH)
        return remote(dq_buf.at[:, cols], dq_out.at[0, :, cols], dqs.at[g], dqr.at[g], behind)

    def compute(g):
        for lo in range(ROWS - 1):
            @pl.when(lo < y)
            def _(lo=lo):
                far_copy(g, lo, lo + 1).wait_recv()
        @pl.when(y > 0)
        def _():
            first_copy(g, 1).wait_recv()
        for s in range(LIST):
            if s == 0:
                both = rowkv[g][z]
            else:
                both = pick(g, s)
            kc[s * BLOCK:(s + 1) * BLOCK] = both[:BLOCK]
            vc[s * BLOCK:(s + 1) * BLOCK] = both[BLOCK:]
        kt[...] = kc[...].T
        dk_acc[...] = jnp.zeros_like(dk_acc)
        dv_acc[...] = jnp.zeros_like(dv_acc)
        diag = mask0[...] > 0.0
        diag2 = jnp.concatenate([diag, diag], axis=1)
        open_slot = [None] + [
            jnp.where((s < count) & (own_id[s] < blk), 0.0, NEG_FILL) for s in range(1, LIST)
        ]

        @pl.loop(0, PER_GROUP // 2)
        def _(pair):
            lo = pl.multiple_of(g * GROUP_WIDTH + pair * 2 * HEAD, HEAD)
            first, second = pl.ds(lo, HEAD), pl.ds(pl.multiple_of(lo + HEAD, HEAD), HEAD)
            qp = jnp.concatenate([q_buf[:, first], q_buf[:, second]], axis=0)
            gp = jnp.concatenate([g_buf[:, first], g_buf[:, second]], axis=0)
            nt = (((1,), (1,)), ((), ()))
            s_all = lax.dot_general(kc[...], qp, nt, preferred_element_type=jnp.float32) * EXP2_SCALE
            dp = lax.dot_general(vc[...], gp, nt, preferred_element_type=jnp.float32)
            parts = [jnp.where(diag2, s_all[:BLOCK], NEG_FILL)]
            for s in range(1, LIST):
                parts.append(s_all[s * BLOCK:(s + 1) * BLOCK] + open_slot[s])
            s_all = jnp.concatenate(parts, axis=0)
            top = jnp.max(s_all, axis=0, keepdims=True)
            w = jnp.exp2(s_all - top)
            p = w * (1.0 / jnp.sum(w, axis=0, keepdims=True))
            delta = jnp.sum(p * dp, axis=0, keepdims=True)
            ds = (p * (dp - delta)).astype(jnp.bfloat16)
            ph = p.astype(jnp.bfloat16)
            dk_acc[...] += jnp.dot(ds, qp, preferred_element_type=jnp.float32)
            dv_acc[...] += jnp.dot(ph, gp, preferred_element_type=jnp.float32)
            dqt = jnp.dot(kt[...], ds, preferred_element_type=jnp.float32) * SCALE
            dq = dqt.T.astype(jnp.bfloat16)
            dq_buf[:, first] = dq[:BLOCK]
            dq_buf[:, second] = dq[BLOCK:]

        dq_copy(g).start()
        for s in range(1, LIST):
            rows = slice(s * BLOCK, (s + 1) * BLOCK)
            y_send[g, s - 1, :BLOCK] = (dk_acc[rows] * SCALE).astype(jnp.bfloat16)
            y_send[g, s - 1, BLOCK:] = dv_acc[rows].astype(jnp.bfloat16)
        for hi in range(1, ROWS):
            @pl.when(y == hi)
            def _(hi=hi):
                for lo in range(hi):
                    y_copy(g, lo, hi).start()
        for t in range(COLS):
            this = y * COLS + t
            for half, (acc, factor) in enumerate(((dk_acc, SCALE), (dv_acc, 1.0))):
                total = jnp.zeros((BLOCK, HEAD), jnp.float32)
                for s in range(LIST):
                    total += jnp.where(own_id[s] == this, acc[s * BLOCK:(s + 1) * BLOCK], 0.0)
                row_acc[g, t, half * BLOCK:(half + 1) * BLOCK] = total * factor

    def add_rows(g):
        for hi in range(1, ROWS):
            @pl.when(hi > y)
            def _(hi=hi):
                @pl.when(y == 0)
                def _():
                    y_copy(g, 0, hi).wait_recv()
                @pl.when(y > 0)
                def _():
                    y_copy(g, 1, hi).wait_recv()
                for t in range(COLS):
                    total = row_acc[g, t]
                    for s in (2, 3):
                        hit = id_smem[hi, s, 0] == y * COLS + t
                        total += jnp.where(hit, y_in[g, hi - 1, s - 1].astype(jnp.float32), 0.0)
                    row_acc[g, t] = total
                @pl.when(y == 0)
                def _():
                    row_acc[g, 0] += y_in[g, hi - 1, 0].astype(jnp.float32)

    def l_copy(g, t):
        return remote(l_send.at[g, t], l_in.at[g, t], ls.at[g, t], lr.at[g, t], at(y, z - 1))

    def r_copy(g, t):
        return remote(r_send.at[g, t], r_in.at[g, t], rs.at[g, t], rr.at[g, t], at(y, z + 1))

    def reduce_row(g, step):
        for zz in range(COLS):
            @pl.when(z == zz)
            def _(zz=zz):
                if zz == COLS - 1 - step:
                    for t in range(zz):
                        total = row_acc[g, t]
                        if step > 0:
                            l_copy(g, t).wait_recv()
                            total += l_in[g, t].astype(jnp.float32)
                        l_send[g, t] = total.astype(jnp.bfloat16)
                        l_copy(g, t).start()
                if zz == step:
                    for t in range(COLS - 1, zz, -1):
                        total = row_acc[g, t]
                        if step > 0:
                            r_copy(g, t).wait_recv()
                            total += r_in[g, t].astype(jnp.float32)
                        r_send[g, t] = total.astype(jnp.bfloat16)
                        r_copy(g, t).start()

    def out_copies(g):
        cols = pl.ds(g * HEAD, HEAD)
        return (
            remote(fin.at[g, pl.ds(0, BLOCK)], dk_out.at[0, :, cols], dks.at[g, 0], dkr.at[g, 0], behind),
            remote(fin.at[g, pl.ds(BLOCK, BLOCK)], dv_out.at[0, :, cols], dks.at[g, 1], dkr.at[g, 1], behind),
        )

    def finish(g):
        for zz in range(COLS):
            @pl.when(z == zz)
            def _(zz=zz):
                total = row_acc[g, zz]
                if zz < COLS - 1:
                    l_copy(g, zz).wait_recv()
                    total += l_in[g, zz].astype(jnp.float32)
                if zz > 0:
                    r_copy(g, zz).wait_recv()
                    total += r_in[g, zz].astype(jnp.float32)
                fin[g] = total.astype(jnp.bfloat16)
        for c in out_copies(g):
            c.start()

    gather_row(0)
    send_listed(0)
    gather_row(1)
    send_listed(1)
    q_copy.wait()
    g_copy.wait()
    compute(0)
    gather_row(2)
    send_listed(2)
    compute(1)
    add_rows(0)
    reduce_row(0, 0)
    gather_row(3)
    send_listed(3)
    compute(2)
    reduce_row(0, 1)
    add_rows(1)
    reduce_row(1, 0)
    reduce_row(0, 2)
    compute(3)
    finish(0)
    reduce_row(1, 1)
    add_rows(2)
    reduce_row(2, 0)
    reduce_row(1, 2)
    reduce_row(2, 1)
    finish(1)
    reduce_row(2, 2)
    add_rows(3)
    reduce_row(3, 0)
    finish(2)
    reduce_row(3, 1)
    reduce_row(3, 2)
    finish(3)

    for g in range(GROUPS):
        dq_copy(g).wait()
        for c in out_copies(g):
            c.wait()
        for zz in range(COLS):
            @pl.when(z == zz)
            def _(g=g, zz=zz):
                for src in range(COLS):
                    if src <= zz < COLS - 1:
                        hop(g, src, 1).wait_send()
                    if src >= zz > 0:
                        hop(g, src, 0).wait_send()
                for t in range(zz):
                    l_copy(g, t).wait_send()
                for t in range(zz + 1, COLS):
                    r_copy(g, t).wait_send()
        for yy in range(ROWS):
            @pl.when(y == yy)
            def _(g=g, yy=yy):
                for hi in range(yy + 1, ROWS):
                    far_copy(g, yy, hi).wait_send()
                    if yy == 0:
                        first_copy(g, hi).wait_send()
                for lo in range(yy):
                    y_copy(g, lo, yy).wait_send()
    for lo in range(ROWS - 1):
        @pl.when(lo < y)
        def _(lo=lo):
            remote(id_tile, id_in.at[y], id_ss.at[lo], id_rs.at[y], at(lo, z)).wait_send()


def per_device(queries, key_heads, value_per_head, out_grads, segment_ids, block_lists, list_counts):
    bf, f32 = jnp.bfloat16, jnp.float32
    anywhere = pl.BlockSpec(memory_space=pl.ANY)
    vmem = pl.BlockSpec(memory_space=pltpu.VMEM)
    smem = pl.BlockSpec(memory_space=pltpu.SMEM)
    two = 2 * BLOCK
    dma = pltpu.SemaphoreType.DMA
    keys_n = LIST * BLOCK
    scratch = (
        [pltpu.VMEM((COLS, two, HEAD), bf)] * GROUPS
        + [pltpu.VMEM((ROWS - 1, 3, two, HEAD), bf)] * GROUPS
        + [
            pltpu.VMEM((8, BLOCK), jnp.int32),
            pltpu.VMEM((ROWS, 8, BLOCK), jnp.int32),
            pltpu.SMEM((ROWS, 8, BLOCK), jnp.int32),
            pltpu.VMEM((BLOCK, QUERY_HEADS * HEAD), bf),
            pltpu.VMEM((BLOCK, QUERY_HEADS * HEAD), bf),
            pltpu.VMEM((GROUPS, ROWS - 1, 2, two, HEAD), bf),
            pltpu.VMEM((BLOCK, BLOCK), f32),
            pltpu.VMEM((keys_n, HEAD), bf),
            pltpu.VMEM((keys_n, HEAD), bf),
            pltpu.VMEM((HEAD, keys_n), bf),
            pltpu.VMEM((keys_n, HEAD), f32),
            pltpu.VMEM((keys_n, HEAD), f32),
            pltpu.VMEM((BLOCK, QUERY_HEADS * HEAD), bf),
            pltpu.VMEM((GROUPS, 3, two, HEAD), bf),
            pltpu.VMEM((GROUPS, ROWS - 1, 3, two, HEAD), bf),
            pltpu.VMEM((GROUPS, COLS, two, HEAD), f32),
            pltpu.VMEM((GROUPS, COLS, two, HEAD), bf),
            pltpu.VMEM((GROUPS, COLS, two, HEAD), bf),
            pltpu.VMEM((GROUPS, COLS, two, HEAD), bf),
            pltpu.VMEM((GROUPS, COLS, two, HEAD), bf),
            pltpu.VMEM((GROUPS, two, HEAD), bf),
            dma((ROWS,)), dma((ROWS,)), dma((ROWS,)), dma((2,)),
            dma((GROUPS, COLS, 2)), dma((GROUPS, COLS)),
            dma((GROUPS, ROWS, ROWS)), dma((GROUPS, ROWS)),
            dma((GROUPS, ROWS)), dma((GROUPS,)),
            dma((GROUPS, ROWS)), dma((GROUPS, ROWS)),
            dma((GROUPS, COLS)), dma((GROUPS, COLS)),
            dma((GROUPS, COLS)), dma((GROUPS, COLS)),
            dma((GROUPS,)), dma((GROUPS,)),
            dma((GROUPS, 2)), dma((GROUPS, 2)),
        ]
    )
    return pl.pallas_call(
        body,
        name="attention_grads",
        out_shape=(
            jax.ShapeDtypeStruct(queries.shape, bf),
            jax.ShapeDtypeStruct(key_heads.shape, bf),
            jax.ShapeDtypeStruct(value_per_head.shape, bf),
        ),
        in_specs=[smem, smem, vmem, vmem, vmem, anywhere, anywhere],
        out_specs=(anywhere, anywhere, anywhere),
        scratch_shapes=scratch,
        compiler_params=pltpu.CompilerParams(
            collective_id=0, has_side_effects=True, vmem_limit_bytes=48 << 20
        ),
    )(
        block_lists.reshape(LIST), list_counts.reshape(1), segment_ids,
        key_heads, value_per_head, queries, out_grads,
    )


def solution(mesh):
    rows = P("section", "blk", None)
    flat = P("section", "blk")
    return jax.shard_map(
        per_device,
        mesh=mesh,
        in_specs=(rows, rows, rows, rows, flat, rows, flat),
        out_specs=(rows, rows, rows),
        check_vma=False,
    )
```

time: 443 us -> 105 us (0.24)
  waiting for transfers between devices: 370 us -> 0 us
  Pallas kernels: 0 us -> 96.2 us
  matrix products: 20.5 us -> 0 us
  between operations: 14.9 us -> 1.31 us
  local copies, waits for them, and re-layouts: 20.4 us -> 7.19 us
  starting transfers between devices: 10.7 us -> 0 us
  other arithmetic: 6.55 us -> 0 us
    reduce_scatter x1 -> x0, waiting for transfers between devices: 179 us -> none  [per_device(): lax.psum_scatter(term_all.reshape(blocks_all * MASK_BLOCK_SIZE, 2 * key_v...]
    all_gather x2 -> x0, waiting for transfers between devices: 165 us -> none  [the longest x1 86.1 us: per_device(): lax.all_gather(value_per_head, 'blk', axis=1, tiled=True)]
    pallas_call x0 -> x1, Pallas kernels: none -> 96.2 us  [per_device(): pl.pallas_call(body, name='attention_grads', out_shape=(jax.ShapeDtypeStr...]
    ppermute x3 -> x0, waiting for transfers between devices: 24.3 us -> none  [from_behind(): lax.ppermute(value, axis, [(i, (i + by) % devices) for i in range(devices)])]
    dot_general x21 -> x0, matrix products: 20.5 us -> none  [the longest x4 5.29 us: group_terms(): jnp.einsum('ihd,ljd->hilj', gradient_row_slice, value_rows, preferred_ele...]
    ppermute x3 -> x0, starting transfers between devices: 10.6 us -> none  [from_behind(): lax.ppermute(value, axis, [(i, (i + by) % devices) for i in range(devices)])]
    dot_general x1 -> x0, local copies, waits for them, and re-layouts: 8.3 us -> none  [per_device(): jnp.einsum('cn,nrw->crw', placement, grad_tiles, precision=lax.Precision....]
  transfers between devices with their start and end apart: 6 -> 0, of which waited for: 5 -> 0; matrix products, arithmetic and copies ran while one was open for 3% -> 0% of each run, Pallas kernels for 0% -> 0%
where the time goes in v1:
time: 105 us
  Pallas kernels  96.2 us (92%)
  local copies, waits for them, and re-layouts  7.19 us (7%)
  between operations  1.31 us (1%)
    pallas_call x1, Pallas kernels, per_device(): pl.pallas_call(body, name='attention_grads', out_shape=(jax.ShapeDtypeStr...  96.2 us
    unnamed x15, local copies, waits for them, and re-layouts  7.19 us

profile of v1, /device:TPU:7, one launch (start us, length us, event | category | flops | bytes accessed | tf_op | source)
XLA Modules:
  0.0 104.7 jit_solution(13780025570526974013)
XLA Ops:
  1.3 0.0 copy-start.4
  1.3 0.0 copy-start.5
  1.3 0.6 copy-done.4
  1.9 0.0 copy-done.5
  2.0 0.0 copy-start
  2.0 1.2 %copy-done = bf16[1,128,4096]{2,1,0:T(8,128)(2,1)S(1)} copy-done((bf16[1,128,4096]{2,1,0:T(8,128)(2,1)S(1)}, bf16[1,128,4096]{2,1,0:T(8,128)(2,1)}, u32[]{:S(2)}) %copy-start) | copy-done | bytes 1048600
  3.2 0.0 copy-start.1
  3.2 1.2 %copy-done.1 = bf16[1,128,4096]{2,1,0:T(8,128)(2,1)S(1)} copy-done((bf16[1,128,4096]{2,1,0:T(8,128)(2,1)S(1)}, bf16[1,128,4096]{2,1,0:T(8,128)(2,1)}, u32[]{:S(2)}) %copy-start.1) | copy-done | bytes 1048600
  4.4 0.0 copy-start.2
  4.4 0.9 copy-done.2
  5.3 0.0 copy-start.3
  5.3 0.9 copy-done.3
  6.2 96.2 %attention_grads.1 = (bf16[1,128,4096]{2,1,0:T(8,128)(2,1)S(1)}, bf16[1,128,512]{2,1,0:T(8,128)(2,1)S(1)}, bf16[1,128,512]{2,1,0:T(8,128)(2,1)S(1)}) custom-call(s32[4]{0:T(128)S(1)} %bitcast.3, s32[1]{0:T(128)} %bitcast.2.counts, s32[1,128]{1,0:T(1,128)S(1)} %copy-done.5, bf16[1,128,512]{2,1,0:T(8,128)(2,1)S(1)} %copy-done.2, ...), custom_call_target="tpu_custom_call" | custom-call | tf_op jit(solution)/shard_map/attention_grads/pallas_call | solution.py:415
  102.4 1.0 copy.14
  103.4 0.7 copy.15
  104.1 0.7 copy.16
Async XLA Ops:
  1.3 0.7 copy-start.4
  1.3 0.7 copy-start.5
  2.0 1.2 %copy-start = (bf16[1,128,4096]{2,1,0:T(8,128)(2,1)S(1)}, bf16[1,128,4096]{2,1,0:T(8,128)(2,1)}, u32[]{:S(2)}) copy-start(bf16[1,128,4096]{2,1,0:T(8,128)(2,1)} %queries.1) | copy-start | bytes 3145732
  3.2 1.2 %copy-start.1 = (bf16[1,128,4096]{2,1,0:T(8,128)(2,1)S(1)}, bf16[1,128,4096]{2,1,0:T(8,128)(2,1)}, u32[]{:S(2)}) copy-start(bf16[1,128,4096]{2,1,0:T(8,128)(2,1)} %grads.1) | copy-start | bytes 3145732
  4.4 0.9 copy-start.2
  5.3 0.9 copy-start.3

commit v2 on v1

--- a/solution.py
+++ b/solution.py
@@ -29,9 +29,9 @@
     row0, row1, row2, row3, far0, far1, far2, far3,
     id_tile, id_in, id_smem,
     q_buf, g_buf, stage, mask0, kc, vc, kt, dk_acc, dv_acc, dq_buf,
-    y_send, y_in, row_acc, l_send, l_in, r_send, r_in, fin,
-    id_ss, id_rs, id_ls, qg_s,
-    zs, zr, ys, yr, bs, br, rys, ryr, ls, lr, rs, rr, dqs, dqr, dks, dkr,
+    y_send, y_in, row_acc, z_send, z_in, fin, transit,
+    id_ss, id_rs, id_ls, qg_s, kv_s,
+    zs, zr, ys, yr, bs, br, rys, ryr, rzs, rzr, dqs, dqr, dks, dkr, trs, trr, tfs,
 ):
     rowkv = (row0, row1, row2, row3)
     far = (far0, far1, far2, far3)
@@ -54,6 +54,26 @@
     behind = (lax.rem(sec + sections - 1, sections), blk)
     ahead = (lax.rem(sec + 1, sections), blk)
 
+    half = sec // 8
+    x = lax.rem(sec, 8) // 2
+    core = lax.rem(sec, 2)
+    wraps = lax.rem(sec, 8) == 0
+    relays = (core == 1) & (x > 0)
+    lands = (core == 1) & (x == 3)
+    relay_from = (half * 8, blk)
+    relay_to = (lax.rem(half + 1, 2) * 8 + 7, blk)
+
+    def relay_at(q):
+        return (half * 8 + 2 * q + 1, blk)
+
+    own_kv = []
+    for g in range(GROUPS):
+        cols = pl.ds(g * HEAD, HEAD)
+        own_kv.append(pltpu.make_async_copy(keys.at[0, :, cols], rowkv[g].at[z, pl.ds(0, BLOCK)], kv_s.at[g, 0]))
+        own_kv.append(pltpu.make_async_copy(values.at[0, :, cols], rowkv[g].at[z, pl.ds(BLOCK, BLOCK)], kv_s.at[g, 1]))
+    for c in own_kv:
+        c.start()
+
     q_copy = pltpu.make_async_copy(queries.at[0], q_buf, qg_s.at[0])
     g_copy = pltpu.make_async_copy(grads.at[0], g_buf, qg_s.at[1])
     q_copy.start()
@@ -61,44 +81,53 @@
 
     barrier = pltpu.get_barrier_semaphore()
     peers = [behind, ahead]
-    for d in (1, 3):
+    for d in (1, 2, 3):
         peers.append(at(y, lax.rem(z + d, COLS)))
     for d in (1, 2, 3):
         peers.append(at(lax.rem(y + d, ROWS), z))
     for p in peers:
         pl.semaphore_signal(barrier, inc=1, device_id=p, device_id_type=MESH)
 
+    @pl.when(wraps)
+    def _():
+        for q in range(1, ROWS):
+            pl.semaphore_signal(barrier, inc=1, device_id=relay_at(q), device_id_type=MESH)
+
+    @pl.when(relays)
+    def _():
+        pl.semaphore_signal(barrier, inc=1, device_id=relay_from, device_id_type=MESH)
+        pl.semaphore_signal(barrier, inc=1, device_id=relay_to, device_id_type=MESH)
+
+    @pl.when(lands)
+    def _():
+        for q in range(1, ROWS):
+            other = (lax.rem(half + 1, 2) * 8 + 2 * q + 1, blk)
+            pl.semaphore_signal(barrier, inc=1, device_id=other, device_id_type=MESH)
+
     lanes = lax.broadcasted_iota(jnp.int32, (8, BLOCK), 0)
     tile = jnp.zeros((8, BLOCK), jnp.int32)
     for s in range(LIST):
         tile = jnp.where(lanes == s, lists[s], tile)
     id_tile[...] = tile
-    for g in range(GROUPS):
-        for zz in range(COLS):
-            @pl.when(z == zz)
-            def _(g=g, zz=zz):
-                rowkv[g][zz, :BLOCK] = keys[0, :, g * HEAD:(g + 1) * HEAD]
-                rowkv[g][zz, BLOCK:] = values[0, :, g * HEAD:(g + 1) * HEAD]
-
-    pl.semaphore_wait(barrier, len(peers))
+    for c in own_kv:
+        c.wait()
+    greeted = len(peers) + jnp.where(wraps | lands, 3, 0) + jnp.where(relays, 2, 0)
+    pl.semaphore_wait(barrier, greeted)
 
     for lo in range(ROWS - 1):
         @pl.when(lo < y)
         def _(lo=lo):
             remote(id_tile, id_in.at[y], id_ss.at[lo], id_rs.at[y], at(lo, z)).start()
 
-    def hop(g, src, to):
-        return remote(rowkv[g].at[src], rowkv[g].at[src], zs.at[g, src, to], zr.at[g, src],
-                      at(y, z + 1) if to else at(y, z - 1))
-
-    for g in range(GROUPS):
-        for zz in range(COLS):
-            @pl.when(z == zz)
-            def _(g=g, zz=zz):
-                if zz < COLS - 1:
-                    hop(g, zz, 1).start()
-                if zz > 0:
-                    hop(g, zz, 0).start()
+    def row_copy(g, d):
+        return remote(rowkv[g].at[z], rowkv[g].at[z], zs.at[g, d], zr.at[g, d],
+                      at(y, lax.rem(z + d, COLS)))
+
+    def start_row(g):
+        for d in range(1, COLS):
+            row_copy(g, d).start()
+
+    start_row(0)
 
     seg_row = jnp.broadcast_to(segs[...].astype(jnp.float32), (BLOCK, BLOCK))
     seg_col = seg_row.T
@@ -106,27 +135,26 @@
     query_pos = lax.broadcasted_iota(jnp.int32, (BLOCK, BLOCK), 1)
     mask0[...] = jnp.where((key_pos <= query_pos) & (seg_row == seg_col), 1.0, 0.0)
 
-    for hi in range(1, ROWS):
-        @pl.when(hi > y)
-        def _(hi=hi):
-            remote(id_tile, id_in.at[hi], id_ss.at[0], id_rs.at[hi], here).wait_recv()
-            c = pltpu.make_async_copy(id_in.at[hi], id_smem.at[hi], id_ls.at[hi])
-            c.start()
-            c.wait()
+    def read_lists():
+        copies = {hi: pltpu.make_async_copy(id_in.at[hi], id_smem.at[hi], id_ls.at[hi]) for hi in range(1, ROWS)}
+        for hi in range(1, ROWS):
+            @pl.when(hi > y)
+            def _(hi=hi):
+                remote(id_tile, id_in.at[hi], id_ss.at[0], id_rs.at[hi], here).wait_recv()
+                copies[hi].start()
+        for hi in range(1, ROWS):
+            @pl.when(hi > y)
+            def _(hi=hi):
+                copies[hi].wait()
 
     own_id = [lists[s] for s in range(LIST)]
     count = counts[0]
 
     def gather_row(g):
-        for zz in range(COLS):
-            @pl.when(z == zz)
-            def _(zz=zz):
-                for dist in range(1, COLS):
-                    for src, onward in ((zz - dist, 1), (zz + dist, 0)):
-                        if 0 <= src < COLS:
-                            hop(g, src, onward).wait_recv()
-                            if onward and zz < COLS - 1 or not onward and zz > 0:
-                                hop(g, src, onward).start()
+        for d in range(1, COLS):
+            row_copy(g, d).wait_recv()
+        if g + 1 < GROUPS:
+            start_row(g + 1)
 
     def far_copy(g, lo, hi):
         return remote(stage.at[g, hi - 1], far[g].at[lo, pl.ds(1, 2)], ys.at[g, lo, hi - 1],
@@ -161,9 +189,34 @@
             y_send.at[g, pl.ds(1, 2)], y_in.at[g, hi - 1, pl.ds(1, 2)])
         return remote(src, dst, rys.at[g, lo], ryr.at[g, hi - 1], at(lo, z))
 
-    def dq_copy(g):
-        cols = pl.ds(g * GROUP_WIDTH, GROUP_WIDTH)
-        return remote(dq_buf.at[:, cols], dq_out.at[0, :, cols], dqs.at[g], dqr.at[g], behind)
+    def dq_copy(g, q, dev):
+        part = (pl.ds(q * 32, 32), pl.ds(g * GROUP_WIDTH, GROUP_WIDTH))
+        return remote(dq_buf.at[part], dq_out.at[(0,) + part], dqs.at[g, q], dqr.at[g, q], dev)
+
+    def spread_copy(g, q):
+        part = (pl.ds(q * 32, 32), pl.ds(g * GROUP_WIDTH, GROUP_WIDTH))
+        return remote(dq_buf.at[part], transit.at[g], dqs.at[g, q], trr.at[g], relay_at(q))
+
+    def pass_copy(g, q):
+        part = (0, pl.ds(q * 32, 32), pl.ds(g * GROUP_WIDTH, GROUP_WIDTH))
+        return remote(transit.at[g], dq_out.at[part], tfs.at[g], dqr.at[g, q], relay_to)
+
+    def send_dq(g):
+        dq_copy(g, 0, behind).start()
+        for q in range(1, ROWS):
+            @pl.when(wraps)
+            def _(q=q):
+                spread_copy(g, q).start()
+            @pl.when(jnp.logical_not(wraps))
+            def _(q=q):
+                dq_copy(g, q, behind).start()
+
+    def pass_on(g):
+        for q in range(1, ROWS):
+            @pl.when(relays & (x == q))
+            def _(q=q):
+                spread_copy(g, q).wait_recv()
+                pass_copy(g, q).start()
 
     def compute(g):
         for lo in range(ROWS - 1):
@@ -215,7 +268,7 @@
             dq_buf[:, first] = dq[:BLOCK]
             dq_buf[:, second] = dq[BLOCK:]
 
-        dq_copy(g).start()
+        send_dq(g)
         for s in range(1, LIST):
             rows = slice(s * BLOCK, (s + 1) * BLOCK)
             y_send[g, s - 1, :BLOCK] = (dk_acc[rows] * SCALE).astype(jnp.bfloat16)
@@ -253,32 +306,14 @@
                 def _():
                     row_acc[g, 0] += y_in[g, hi - 1, 0].astype(jnp.float32)
 
-    def l_copy(g, t):
-        return remote(l_send.at[g, t], l_in.at[g, t], ls.at[g, t], lr.at[g, t], at(y, z - 1))
-
-    def r_copy(g, t):
-        return remote(r_send.at[g, t], r_in.at[g, t], rs.at[g, t], rr.at[g, t], at(y, z + 1))
-
-    def reduce_row(g, step):
-        for zz in range(COLS):
-            @pl.when(z == zz)
-            def _(zz=zz):
-                if zz == COLS - 1 - step:
-                    for t in range(zz):
-                        total = row_acc[g, t]
-                        if step > 0:
-                            l_copy(g, t).wait_recv()
-                            total += l_in[g, t].astype(jnp.float32)
-                        l_send[g, t] = total.astype(jnp.bfloat16)
-                        l_copy(g, t).start()
-                if zz == step:
-                    for t in range(COLS - 1, zz, -1):
-                        total = row_acc[g, t]
-                        if step > 0:
-                            r_copy(g, t).wait_recv()
-                            total += r_in[g, t].astype(jnp.float32)
-                        r_send[g, t] = total.astype(jnp.bfloat16)
-                        r_copy(g, t).start()
+    def reduce_copy(g, d):
+        return remote(z_send.at[g, d - 1], z_in.at[g, d - 1], rzs.at[g, d], rzr.at[g, d],
+                      at(y, lax.rem(z + d, COLS)))
+
+    def send_row(g):
+        for d in range(1, COLS):
+            z_send[g, d - 1] = row_acc[g, lax.rem(z + d, COLS)].astype(jnp.bfloat16)
+            reduce_copy(g, d).start()
 
     def out_copies(g):
         cols = pl.ds(g * HEAD, HEAD)
@@ -288,21 +323,16 @@
         )
 
     def finish(g):
-        for zz in range(COLS):
-            @pl.when(z == zz)
-            def _(zz=zz):
-                total = row_acc[g, zz]
-                if zz < COLS - 1:
-                    l_copy(g, zz).wait_recv()
-                    total += l_in[g, zz].astype(jnp.float32)
-                if zz > 0:
-                    r_copy(g, zz).wait_recv()
-                    total += r_in[g, zz].astype(jnp.float32)
-                fin[g] = total.astype(jnp.bfloat16)
+        total = row_acc[g, z]
+        for d in range(1, COLS):
+            reduce_copy(g, d).wait_recv()
+            total += z_in[g, d - 1].astype(jnp.float32)
+        fin[g] = total.astype(jnp.bfloat16)
         for c in out_copies(g):
             c.start()
 
     gather_row(0)
+    read_lists()
     send_listed(0)
     gather_row(1)
     send_listed(1)
@@ -312,47 +342,39 @@
     gather_row(2)
     send_listed(2)
     compute(1)
-    add_rows(0)
-    reduce_row(0, 0)
     gather_row(3)
     send_listed(3)
+    pass_on(0)
+    add_rows(0)
+    send_row(0)
     compute(2)
-    reduce_row(0, 1)
+    pass_on(1)
     add_rows(1)
-    reduce_row(1, 0)
-    reduce_row(0, 2)
+    send_row(1)
+    finish(0)
     compute(3)
-    finish(0)
-    reduce_row(1, 1)
+    pass_on(2)
     add_rows(2)
-    reduce_row(2, 0)
-    reduce_row(1, 2)
-    reduce_row(2, 1)
+    send_row(2)
     finish(1)
-    reduce_row(2, 2)
+    pass_on(3)
+    finish(2)
     add_rows(3)
-    reduce_row(3, 0)
-    finish(2)
-    reduce_row(3, 1)
-    reduce_row(3, 2)
+    send_row(3)
     finish(3)
 
     for g in range(GROUPS):
-        dq_copy(g).wait()
+        for q in range(ROWS):
+            dq_copy(g, q, behind).wait()
+        for q in range(1, ROWS):
+            @pl.when(relays & (x == q))
+            def _(g=g, q=q):
+                pass_copy(g, q).wait_send()
         for c in out_copies(g):
             c.wait()
-        for zz in range(COLS):
-            @pl.when(z == zz)
-            def _(g=g, zz=zz):
-                for src in range(COLS):
-                    if src <= zz < COLS - 1:
-                        hop(g, src, 1).wait_send()
-                    if src >= zz > 0:
-                        hop(g, src, 0).wait_send()
-                for t in range(zz):
-                    l_copy(g, t).wait_send()
-                for t in range(zz + 1, COLS):
-                    r_copy(g, t).wait_send()
+        for d in range(1, COLS):
+            row_copy(g, d).wait_send()
+            reduce_copy(g, d).wait_send()
         for yy in range(ROWS):
             @pl.when(y == yy)
             def _(g=g, yy=yy):
@@ -396,20 +418,19 @@
             pltpu.VMEM((GROUPS, 3, two, HEAD), bf),
             pltpu.VMEM((GROUPS, ROWS - 1, 3, two, HEAD), bf),
             pltpu.VMEM((GROUPS, COLS, two, HEAD), f32),
-            pltpu.VMEM((GROUPS, COLS, two, HEAD), bf),
-            pltpu.VMEM((GROUPS, COLS, two, HEAD), bf),
-            pltpu.VMEM((GROUPS, COLS, two, HEAD), bf),
-            pltpu.VMEM((GROUPS, COLS, two, HEAD), bf),
+            pltpu.VMEM((GROUPS, COLS - 1, two, HEAD), bf),
+            pltpu.VMEM((GROUPS, COLS - 1, two, HEAD), bf),
             pltpu.VMEM((GROUPS, two, HEAD), bf),
-            dma((ROWS,)), dma((ROWS,)), dma((ROWS,)), dma((2,)),
-            dma((GROUPS, COLS, 2)), dma((GROUPS, COLS)),
+            pltpu.VMEM((GROUPS, BLOCK // 4, GROUP_WIDTH), bf),
+            dma((ROWS,)), dma((ROWS,)), dma((ROWS,)), dma((2,)), dma((GROUPS, 2)),
+            dma((GROUPS, COLS)), dma((GROUPS, COLS)),
             dma((GROUPS, ROWS, ROWS)), dma((GROUPS, ROWS)),
             dma((GROUPS, ROWS)), dma((GROUPS,)),
             dma((GROUPS, ROWS)), dma((GROUPS, ROWS)),
             dma((GROUPS, COLS)), dma((GROUPS, COLS)),
-            dma((GROUPS, COLS)), dma((GROUPS, COLS)),
-            dma((GROUPS,)), dma((GROUPS,)),
+            dma((GROUPS, 4)), dma((GROUPS, 4)),
             dma((GROUPS, 2)), dma((GROUPS, 2)),
+            dma((GROUPS,)), dma((GROUPS,)), dma((GROUPS,)),
         ]
     )
     return pl.pallas_call(
@@ -420,11 +441,11 @@
             jax.ShapeDtypeStruct(key_heads.shape, bf),
             jax.ShapeDtypeStruct(value_per_head.shape, bf),
         ),
-        in_specs=[smem, smem, vmem, vmem, vmem, anywhere, anywhere],
+        in_specs=[smem, smem, vmem, anywhere, anywhere, anywhere, anywhere],
         out_specs=(anywhere, anywhere, anywhere),
         scratch_shapes=scratch,
         compiler_params=pltpu.CompilerParams(
-            collective_id=0, has_side_effects=True, vmem_limit_bytes=48 << 20
+            collective_id=0, has_side_effects=True, vmem_limit_bytes=62 << 20
         ),
     )(
         block_lists.reshape(LIST), list_counts.reshape(1), segment_ids,

time: 105 us -> 89.3 us (0.85)
  Pallas kernels: 96.2 us -> 83.9 us
  local copies, waits for them, and re-layouts: 7.19 us -> 3.93 us
    pallas_call x1, Pallas kernels: 96.2 us -> 83.9 us  [per_device(): pl.pallas_call(body, name='attention_grads', out_shape=(jax.ShapeDtypeStr...]
    unnamed x15 -> x7, local copies, waits for them, and re-layouts: 7.19 us -> 3.93 us
where the time goes in v2:
time: 89.3 us; the launch traced here: 89.1 us
  Pallas kernels  83.9 us (94%)
  local copies, waits for them, and re-layouts  3.93 us (4%)
  between operations  1.3 us (1%)
    pallas_call x1, Pallas kernels, per_device(): pl.pallas_call(body, name='attention_grads', out_shape=(jax.ShapeDtypeStr...  83.9 us
    unnamed x7, local copies, waits for them, and re-layouts  3.93 us

profile of v2, /device:TPU:7, one launch (start us, length us, event | category | flops | bytes accessed | tf_op | source)
XLA Modules:
  0.0 89.1 jit_solution(6114775230352576439)
XLA Ops:
  1.3 83.9 %attention_grads.1 = (bf16[1,128,4096]{2,1,0:T(8,128)(2,1)}, bf16[1,128,512]{2,1,0:T(8,128)(2,1)}, bf16[1,128,512]{2,1,0:T(8,128)(2,1)}) custom-call(s32[4]{0:T(128)} %bitcast.3, s32[1]{0:T(128)} %bitcast.2.counts, s32[1,128]{1,0:T(1,128)} %segs.1, bf16[1,128,512]{2,1,0:T(8,128)(2,1)} %keys.1, bf16[1,128,512]{2,1,0:T(8,128)(2,1)} %values.1, ...), custom_call_target="tpu_custom_call" | custom-call | tf_op jit(solution)/shard_map/attention_grads/pallas_call | solution.py:436
  85.2 0.0 copy-start.1
  85.2 2.3 %copy.14 = bf16[1,128,4096]{2,1,0:T(8,128)(2,1)} copy(bf16[1,128,4096]{2,1,0:T(8,128)(2,1)} %get-tuple-element.6) | data formatting | bytes 2097152
  87.5 0.0 copy-done.1
  87.5 0.0 copy-start
  87.5 0.7 copy.15
  88.2 0.3 copy-done
  88.5 0.7 copy.16
Async XLA Ops:
  85.2 2.3 %copy-start.1 = (bf16[1,128,512]{2,1,0:T(8,128)(2,1)S(1)}, bf16[1,128,512]{2,1,0:T(8,128)(2,1)}, u32[]{:S(2)}) copy-start(bf16[1,128,512]{2,1,0:T(8,128)(2,1)} %get-tuple-element.7) | copy-start | bytes 393220
  87.5 1.0 %copy-start = (bf16[1,128,512]{2,1,0:T(8,128)(2,1)S(1)}, bf16[1,128,512]{2,1,0:T(8,128)(2,1)}, u32[]{:S(2)}) copy-start(bf16[1,128,512]{2,1,0:T(8,128)(2,1)} %get-tuple-element.8) | copy-start | bytes 393220

commit v3 on v2

--- a/solution.py
+++ b/solution.py
@@ -29,9 +29,10 @@
     row0, row1, row2, row3, far0, far1, far2, far3,
     id_tile, id_in, id_smem,
     q_buf, g_buf, stage, mask0, kc, vc, kt, dk_acc, dv_acc, dq_buf,
-    y_send, y_in, row_acc, z_send, z_in, fin, transit,
+    y_send, y_in, row_acc, z_send, z_in, fin, transit, lead_in, lead_out,
     id_ss, id_rs, id_ls, qg_s, kv_s,
     zs, zr, ys, yr, bs, br, rys, ryr, rzs, rzr, dqs, dqr, dks, dkr, trs, trr, tfs,
+    lis, lir, los, lor,
 ):
     rowkv = (row0, row1, row2, row3)
     far = (far0, far1, far2, far3)
@@ -163,10 +164,19 @@
     def first_copy(g, hi):
         return remote(rowkv[g].at[0], far[g].at[0, 0], bs.at[g, hi - 1], br.at[g], at(hi, z))
 
+    def hand_copy(g):
+        return remote(far[g].at[0, 0], far[g].at[0, 0], bs.at[g, 1], br.at[g], at(2, z))
+
+    def hand_first(g):
+        @pl.when(y == 1)
+        def _():
+            first_copy(g, 1).wait_recv()
+            hand_copy(g).start()
+
     def send_listed(g):
         @pl.when(y == 0)
         def _():
-            for hi in range(1, ROWS):
+            for hi in (1, 3):
                 first_copy(g, hi).start()
         for lo in range(ROWS - 1):
             @pl.when(y == lo)
@@ -184,10 +194,27 @@
         away = far[g][jnp.minimum(r, ROWS - 2), s - 1]
         return jnp.where(r == y, near, away)
 
+    def direct(g, hi):
+        return hi == 3
+
     def y_copy(g, lo, hi):
-        src, dst = (y_send.at[g], y_in.at[g, hi - 1]) if lo == 0 else (
+        src, dst = (y_send.at[g], y_in.at[g, hi - 1]) if lo == 0 and direct(g, hi) else (
             y_send.at[g, pl.ds(1, 2)], y_in.at[g, hi - 1, pl.ds(1, 2)])
         return remote(src, dst, rys.at[g, lo], ryr.at[g, hi - 1], at(lo, z))
+
+    def lead_copy(g):
+        return remote(y_send.at[g, 0], lead_in.at[g], lis.at[g], lir.at[g], at(1, z))
+
+    def lead_end_copy(g):
+        return remote(lead_out.at[g], y_in.at[g, 0, 0], los.at[g], lor.at[g], at(0, z))
+
+    def fold_first(g):
+        @pl.when(y == 1)
+        def _():
+            lead_copy(g).wait_recv()
+            total = y_send[g, 0].astype(jnp.float32) + lead_in[g].astype(jnp.float32)
+            lead_out[g] = total.astype(jnp.bfloat16)
+            lead_end_copy(g).start()
 
     def dq_copy(g, q, dev):
         part = (pl.ds(q * 32, 32), pl.ds(g * GROUP_WIDTH, GROUP_WIDTH))
@@ -201,15 +228,43 @@
         part = (0, pl.ds(q * 32, 32), pl.ds(g * GROUP_WIDTH, GROUP_WIDTH))
         return remote(transit.at[g], dq_out.at[part], tfs.at[g], dqr.at[g, q], relay_to)
 
+    def whole_copy(g):
+        cols = pl.ds(g * GROUP_WIDTH, GROUP_WIDTH)
+        return remote(dq_buf.at[:, cols], dq_out.at[0, :, cols], dqs.at[g, 0], dqr.at[g, 0], behind)
+
     def send_dq(g):
-        dq_copy(g, 0, behind).start()
+        @pl.when(wraps)
+        def _():
+            for q in range(1, ROWS):
+                spread_copy(g, q).start()
+            dq_copy(g, 0, behind).start()
+
+        @pl.when(jnp.logical_not(wraps))
+        def _():
+            whole_copy(g).start()
+
+    def drain_dq(g):
+        @pl.when(wraps)
+        def _():
+            for q in range(ROWS):
+                dq_copy(g, q, behind).wait_send()
+
+        @pl.when(jnp.logical_not(wraps))
+        def _():
+            whole_copy(g).wait_send()
+
+        @pl.when(lands)
+        def _():
+            for q in range(ROWS):
+                dq_copy(g, q, behind).wait_recv()
+
+        @pl.when(jnp.logical_not(lands))
+        def _():
+            whole_copy(g).wait_recv()
         for q in range(1, ROWS):
-            @pl.when(wraps)
+            @pl.when(relays & (x == q))
             def _(q=q):
-                spread_copy(g, q).start()
-            @pl.when(jnp.logical_not(wraps))
-            def _(q=q):
-                dq_copy(g, q, behind).start()
+                pass_copy(g, q).wait_send()
 
     def pass_on(g):
         for q in range(1, ROWS):
@@ -223,7 +278,7 @@
             @pl.when(lo < y)
             def _(lo=lo):
                 far_copy(g, lo, lo + 1).wait_recv()
-        @pl.when(y > 0)
+        @pl.when(y > 1)
         def _():
             first_copy(g, 1).wait_recv()
         for s in range(LIST):
@@ -242,7 +297,7 @@
             jnp.where((s < count) & (own_id[s] < blk), 0.0, NEG_FILL) for s in range(1, LIST)
         ]
 
-        @pl.loop(0, PER_GROUP // 2)
+        @pl.loop(0, PER_GROUP // 2, unroll=True)
         def _(pair):
             lo = pl.multiple_of(g * GROUP_WIDTH + pair * 2 * HEAD, HEAD)
             first, second = pl.ds(lo, HEAD), pl.ds(pl.multiple_of(lo + HEAD, HEAD), HEAD)
@@ -268,7 +323,6 @@
             dq_buf[:, first] = dq[:BLOCK]
             dq_buf[:, second] = dq[BLOCK:]
 
-        send_dq(g)
         for s in range(1, LIST):
             rows = slice(s * BLOCK, (s + 1) * BLOCK)
             y_send[g, s - 1, :BLOCK] = (dk_acc[rows] * SCALE).astype(jnp.bfloat16)
@@ -276,8 +330,11 @@
         for hi in range(1, ROWS):
             @pl.when(y == hi)
             def _(hi=hi):
+                if hi == 2 and not direct(g, hi):
+                    lead_copy(g).start()
                 for lo in range(hi):
                     y_copy(g, lo, hi).start()
+        send_dq(g)
         for t in range(COLS):
             this = y * COLS + t
             for half, (acc, factor) in enumerate(((dk_acc, SCALE), (dv_acc, 1.0))):
@@ -293,6 +350,8 @@
                 @pl.when(y == 0)
                 def _():
                     y_copy(g, 0, hi).wait_recv()
+                    if hi == 1 and not direct(g, hi):
+                        lead_end_copy(g).wait_recv()
                 @pl.when(y > 0)
                 def _():
                     y_copy(g, 1, hi).wait_recv()
@@ -302,9 +361,10 @@
                         hit = id_smem[hi, s, 0] == y * COLS + t
                         total += jnp.where(hit, y_in[g, hi - 1, s - 1].astype(jnp.float32), 0.0)
                     row_acc[g, t] = total
-                @pl.when(y == 0)
-                def _():
-                    row_acc[g, 0] += y_in[g, hi - 1, 0].astype(jnp.float32)
+                if hi != 2 or direct(g, hi):
+                    @pl.when(y == 0)
+                    def _():
+                        row_acc[g, 0] += y_in[g, hi - 1, 0].astype(jnp.float32)
 
     def reduce_copy(g, d):
         return remote(z_send.at[g, d - 1], z_in.at[g, d - 1], rzs.at[g, d], rzr.at[g, d],
@@ -331,63 +391,99 @@
         for c in out_copies(g):
             c.start()
 
+    def drain_in(g):
+        for d in range(1, COLS):
+            row_copy(g, d).wait_send()
+        for yy in range(ROWS):
+            @pl.when(y == yy)
+            def _(yy=yy):
+                for hi in range(yy + 1, ROWS):
+                    far_copy(g, yy, hi).wait_send()
+                    if yy == 0 and hi != 2:
+                        first_copy(g, hi).wait_send()
+                if yy == 1:
+                    hand_copy(g).wait_send()
+
+    def drain_slots(g):
+        for yy in range(1, ROWS):
+            @pl.when(y == yy)
+            def _(yy=yy):
+                if yy == 1 and not direct(g, yy):
+                    lead_end_copy(g).wait_send()
+                if yy == 2 and not direct(g, yy):
+                    lead_copy(g).wait_send()
+                for lo in range(yy):
+                    y_copy(g, lo, yy).wait_send()
+
+    def drain_row(g):
+        for d in range(1, COLS):
+            reduce_copy(g, d).wait_send()
+
+    def drain_out(g):
+        for c in out_copies(g):
+            c.wait()
+
+    def drain_lists():
+        for lo in range(ROWS - 1):
+            @pl.when(lo < y)
+            def _(lo=lo):
+                remote(id_tile, id_in.at[y], id_ss.at[lo], id_rs.at[y], at(lo, z)).wait_send()
+
     gather_row(0)
     read_lists()
     send_listed(0)
+    hand_first(0)
     gather_row(1)
     send_listed(1)
     q_copy.wait()
     g_copy.wait()
     compute(0)
+    hand_first(1)
     gather_row(2)
     send_listed(2)
     compute(1)
+    hand_first(2)
+    fold_first(0)
     gather_row(3)
     send_listed(3)
     pass_on(0)
     add_rows(0)
     send_row(0)
     compute(2)
+    hand_first(3)
+    fold_first(1)
     pass_on(1)
+    compute(3)
+    fold_first(2)
     add_rows(1)
     send_row(1)
     finish(0)
-    compute(3)
     pass_on(2)
     add_rows(2)
     send_row(2)
     finish(1)
+    fold_first(3)
     pass_on(3)
     finish(2)
+    drain_lists()
+    for g in range(GROUPS):
+        drain_in(g)
+    for g in range(GROUPS - 1):
+        drain_slots(g)
     add_rows(3)
     send_row(3)
+    drain_slots(3)
+    for g in range(GROUPS - 1):
+        drain_dq(g)
+        drain_row(g)
+    for g in range(GROUPS - 2):
+        drain_out(g)
     finish(3)
 
-    for g in range(GROUPS):
-        for q in range(ROWS):
-            dq_copy(g, q, behind).wait()
-        for q in range(1, ROWS):
-            @pl.when(relays & (x == q))
-            def _(g=g, q=q):
-                pass_copy(g, q).wait_send()
-        for c in out_copies(g):
-            c.wait()
-        for d in range(1, COLS):
-            row_copy(g, d).wait_send()
-            reduce_copy(g, d).wait_send()
-        for yy in range(ROWS):
-            @pl.when(y == yy)
-            def _(g=g, yy=yy):
-                for hi in range(yy + 1, ROWS):
-                    far_copy(g, yy, hi).wait_send()
-                    if yy == 0:
-                        first_copy(g, hi).wait_send()
-                for lo in range(yy):
-                    y_copy(g, lo, yy).wait_send()
-    for lo in range(ROWS - 1):
-        @pl.when(lo < y)
-        def _(lo=lo):
-            remote(id_tile, id_in.at[y], id_ss.at[lo], id_rs.at[y], at(lo, z)).wait_send()
+    drain_dq(3)
+    drain_row(3)
+    drain_out(2)
+    drain_out(3)
 
 
 def per_device(queries, key_heads, value_per_head, out_grads, segment_ids, block_lists, list_counts):
@@ -422,6 +518,8 @@
             pltpu.VMEM((GROUPS, COLS - 1, two, HEAD), bf),
             pltpu.VMEM((GROUPS, two, HEAD), bf),
             pltpu.VMEM((GROUPS, BLOCK // 4, GROUP_WIDTH), bf),
+            pltpu.VMEM((GROUPS, two, HEAD), bf),
+            pltpu.VMEM((GROUPS, two, HEAD), bf),
             dma((ROWS,)), dma((ROWS,)), dma((ROWS,)), dma((2,)), dma((GROUPS, 2)),
             dma((GROUPS, COLS)), dma((GROUPS, COLS)),
             dma((GROUPS, ROWS, ROWS)), dma((GROUPS, ROWS)),
@@ -431,6 +529,7 @@
             dma((GROUPS, 4)), dma((GROUPS, 4)),
             dma((GROUPS, 2)), dma((GROUPS, 2)),
             dma((GROUPS,)), dma((GROUPS,)), dma((GROUPS,)),
+            dma((GROUPS,)), dma((GROUPS,)), dma((GROUPS,)), dma((GROUPS,)),
         ]
     )
     return pl.pallas_call(
@@ -445,11 +544,12 @@
         out_specs=(anywhere, anywhere, anywhere),
         scratch_shapes=scratch,
         compiler_params=pltpu.CompilerParams(
-            collective_id=0, has_side_effects=True, vmem_limit_bytes=62 << 20
+            collective_id=0, has_side_effects=True, vmem_limit_bytes=48 << 20
         ),
     )(
         block_lists.reshape(LIST), list_counts.reshape(1), segment_ids,
-        key_heads, value_per_head, queries, out_grads,
+        *(pltpu.with_memory_space_constraint(a, pltpu.HBM)
+          for a in (key_heads, value_per_head, queries, out_grads)),
     )
 
 

time: 89.3 us -> 82.9 us (0.928)
  Pallas kernels: 83.9 us -> 78.5 us
  local copies, waits for them, and re-layouts: 3.93 us -> 2.94 us
    pallas_call x1, Pallas kernels: 83.9 us -> 78.5 us  [per_device(): pl.pallas_call(body, name='attention_grads', out_shape=(jax.ShapeDtypeStr...]
    unnamed x7, local copies, waits for them, and re-layouts: 3.93 us -> 2.94 us
where the time goes in v3:
time: 82.9 us; the launch traced here: 82.7 us
  Pallas kernels  78.5 us (95%)
  local copies, waits for them, and re-layouts  2.94 us (4%)
  between operations  1.31 us (2%)
    pallas_call x1, Pallas kernels, per_device(): pl.pallas_call(body, name='attention_grads', out_shape=(jax.ShapeDtypeStr...  78.5 us
    unnamed x7, local copies, waits for them, and re-layouts  2.94 us

profile of v3, /device:TPU:7, one launch (start us, length us, event | category | flops | bytes accessed | tf_op | source)
XLA Modules:
  0.0 82.7 jit_solution(17593499578771847970)
XLA Ops:
  1.3 0.0 copy-start
  1.3 0.0 copy-start.1
  1.3 0.6 copy-done
  1.9 0.0 copy-done.1
  2.0 78.5 %attention_grads.1 = (bf16[1,128,4096]{2,1,0:T(8,128)(2,1)S(1)}, bf16[1,128,512]{2,1,0:T(8,128)(2,1)S(1)}, bf16[1,128,512]{2,1,0:T(8,128)(2,1)S(1)}) custom-call(s32[4]{0:T(128)S(1)} %bitcast.3, s32[1]{0:T(128)} %bitcast.2.counts, s32[1,128]{1,0:T(1,128)S(1)} %copy-done.1, bf16[1,128,512]{2,1,0:T(8,128)(2,1)} %keys.1, bf16[1,128,512]{2,1,0:T(8,128)(2,1)} %values.1, ...), custom_call_target="tpu_custom_call" | custom-call | tf_op jit(solution)/shard_map/attention_grads/pallas_call | solution.py:535
  80.5 1.0 %copy.14 = bf16[1,128,4096]{2,1,0:T(8,128)(2,1)} copy(bf16[1,128,4096]{2,1,0:T(8,128)(2,1)S(1)} %get-tuple-element.6) | data formatting | bytes 2097152
  81.4 0.7 copy.15
  82.1 0.7 copy.16
Async XLA Ops:
  1.3 0.7 copy-start
  1.3 0.7 copy-start.1

commit v4 on v3

--- a/solution.py
+++ b/solution.py
@@ -461,8 +461,8 @@
     pass_on(2)
     add_rows(2)
     send_row(2)
+    fold_first(3)
     finish(1)
-    fold_first(3)
     pass_on(3)
     finish(2)
     drain_lists()

time: 82.9 us -> 82.8 us (level)
  no operation moved by 1% of the time
where the time goes in v4:
time: 82.8 us; the launch traced here: 82.7 us
  Pallas kernels  78.5 us (95%)
  local copies, waits for them, and re-layouts  2.94 us (4%)
  between operations  1.31 us (2%)
    pallas_call x1, Pallas kernels, per_device(): pl.pallas_call(body, name='attention_grads', out_shape=(jax.ShapeDtypeStr...  78.5 us
    unnamed x7, local copies, waits for them, and re-layouts  2.94 us

profile of v4, /device:TPU:7, one launch (start us, length us, event | category | flops | bytes accessed | tf_op | source)
XLA Modules:
  0.0 82.7 jit_solution(17048017416460857432)
XLA Ops:
  1.3 0.0 copy-start
  1.3 0.0 copy-start.1
  1.3 0.6 copy-done
  1.9 0.0 copy-done.1
  2.0 78.5 %attention_grads.1 = (bf16[1,128,4096]{2,1,0:T(8,128)(2,1)S(1)}, bf16[1,128,512]{2,1,0:T(8,128)(2,1)S(1)}, bf16[1,128,512]{2,1,0:T(8,128)(2,1)S(1)}) custom-call(s32[4]{0:T(128)S(1)} %bitcast.3, s32[1]{0:T(128)} %bitcast.2.counts, s32[1,128]{1,0:T(1,128)S(1)} %copy-done.1, bf16[1,128,512]{2,1,0:T(8,128)(2,1)} %keys.1, bf16[1,128,512]{2,1,0:T(8,128)(2,1)} %values.1, ...), custom_call_target="tpu_custom_call" | custom-call | tf_op jit(solution)/shard_map/attention_grads/pallas_call | solution.py:535
  80.4 1.0 %copy.14 = bf16[1,128,4096]{2,1,0:T(8,128)(2,1)} copy(bf16[1,128,4096]{2,1,0:T(8,128)(2,1)S(1)} %get-tuple-element.6) | data formatting | bytes 2097152
  81.4 0.7 copy.15
  82.0 0.7 copy.16
Async XLA Ops:
  1.3 0.7 copy-start
  1.3 0.7 copy-start.1
